TPU v7x, 32 devices: a whole 2x2x4 slice. The times are simulated.
32 devices in a mesh: row: 16 (over z, x, core), col: 2 (over y).
Axes of the slice: x: 2, y: 2, z: 4, core: 2. Of those that a mesh axis runs over, the one named last changes fastest.
Arguments:
- matrix_panel: bfloat16 [128, 131072], P('col', 'row'), may hold values from -6 to 6
- row_signs: int32 [131072], P('row'), may hold values from -1 to 1, as said below
- sample_rows: int32 [2048], replicated, may hold values from 0 to 131071, as said below
Outputs:
- sketch: float32 [128, 2048], P('col', 'row')
- gram: float32 [128, 128], P('col')
Inputs may be any that keep to these rules, and one draw needn't show every extreme that they name: `row_signs`: each entry is -1 or +1. `sample_rows`: strictly increasing, so all distinct.
All inputs are finite; a program needn't handle non-finite values.
Results may differ from a plain program's by a relative error of at most 0.0003.
Values sent between devices are 32-bit elements; how exact they have to be, the bound alone decides.
No kernel may reach another device: no remote copies, remote signals or barrier semaphores. Data moves between devices by JAX's collectives and lax.ppermute only.
A program may use at most 64 MiB of HBM per device.

v0:
```python
import jax
import jax.numpy as jnp
from jax import lax
from jax.sharding import PartitionSpec as P


def parity_sign(left, right, bit_count):
    common = jnp.bitwise_and(left, right)
    total = jnp.zeros_like(common)
    for bit_index in range(bit_count):
        total = total + jnp.bitwise_and(jnp.right_shift(common, bit_index), 1)
    return (1 - 2 * jnp.bitwise_and(total, 1)).astype(jnp.float32)


def hadamard(order_size):
    bit_count = order_size.bit_length() - 1
    row_index = jnp.arange(order_size, dtype=jnp.int32)
    return parity_sign(row_index[:, None], row_index[None, :], bit_count)


def local_mix(block, signs):
    columns, length = block.shape
    first_size = min(length, 256)
    second_size = length // first_size
    values = block.astype(jnp.float32) * signs.astype(jnp.float32)[None, :]
    values = values.reshape(columns, first_size, second_size)
    values = jnp.einsum(
        "cab,ad->cdb", values, hadamard(first_size), precision=lax.Precision.HIGHEST
    )
    values = jnp.einsum(
        "cdb,be->cde", values, hadamard(second_size), precision=lax.Precision.HIGHEST
    )
    return values.reshape(columns, length) / jnp.sqrt(jnp.float32(length))


def body(matrix_panel, row_signs, sample_rows):
    devices = lax.axis_size("row")
    position = lax.axis_index("row")
    bit_count = devices.bit_length() - 1
    columns, length = matrix_panel.shape
    everything = sample_rows.shape[0]
    per_device = everything // devices
    mixed = local_mix(matrix_panel, row_signs)
    owner = sample_rows // length
    offset = sample_rows - owner * length
    chosen = jnp.take(mixed, offset, axis=1)
    pieces = chosen.reshape(columns, devices, per_device)
    received = lax.all_to_all(pieces, "row", split_axis=1, concat_axis=1, tiled=True)
    mine = lax.dynamic_slice_in_dim(owner, position * per_device, per_device, 0)
    sources = jnp.arange(devices, dtype=jnp.int32)
    table = parity_sign(sources[:, None], mine[None, :], bit_count)
    summed = jnp.sum(received * table[None, :, :], axis=1)
    sketch = summed / jnp.sqrt(jnp.float32(devices))
    gathered = lax.all_gather(sketch, "col", axis=0, tiled=True)
    partial_gram = jnp.dot(gathered, gathered.T, precision=lax.Precision.HIGHEST)
    totals = lax.psum(partial_gram, "row")
    own_rows = lax.dynamic_slice_in_dim(totals, lax.axis_index("col") * columns, columns, 0)
    gram = own_rows / everything
    return (sketch, gram)


def solution(mesh):
    return jax.shard_map(
        body,
        mesh=mesh,
        in_specs=(P("col", "row"), P("row"), P()),
        out_specs=(P("col", "row"), P("col", None)),
        check_vma=False,
    )
```

profile of v0, /device:TPU:8, one launch (start us, length us, event | category | flops | bytes accessed | tf_op | source)
XLA Modules:
  0.0 157.8 jit_solution(18320951381184153002)
XLA Ops:
  7.2 0.7 add_select_fusion
  7.9 0.7 and_bitcast_fusion
  8.6 0.8 convert_element_type.21
  9.4 1.4 convert_multiply_fusion
  10.8 2.7 %copy.13 = f32[64,8192]{0,1:T(8,128)} copy(f32[64,8192]{1,0:T(8,128)S(1)} %convert_multiply_fusion) | data formatting | bytes 4194304 | tf_op jit(solution)/shard_map/mul | solution.py:25
  13.5 4.5 %copy.14 = f32[64,256,32]{1,2,0:T(8,128)S(1)} copy(f32[64,256,32]{0,2,1:T(8,128)} %bitcast.21) | data formatting | bytes 4194304 | tf_op jit(solution)/shard_map/reshape | solution.py:26
  17.9 2.2 %fusion = f32[256,2048]{0,1:S(1)} fusion(f32[256,2048]{0,1:T(8,128)S(1)} %bitcast.22), kind=kOutput, calls=%fused_computation.5 | convolution fusion | flops 1612447744 | bytes 4194304
  20.1 1.9 %convolution_multiply_fusion = f32[64,256,32]{1,2,0:T(8,128)S(1)} fusion(f32[64,256,32]{1,2,0:T(8,128)S(1)} %bitcast.23), kind=kOutput, calls=%fused_computation.2 | convolution fusion | flops 201870336 | bytes 4194304 | tf_op jit(solution)/shard_map/cdb,be->cde/dot_general | solution.py:30
  22.0 4.5 %copy.15 = f32[64,256,32]{0,2,1:T(8,128)} copy(f32[64,256,32]{1,2,0:T(8,128)S(1)} %convolution_multiply_fusion) | data formatting | bytes 4194304 | tf_op jit(solution)/shard_map/div | solution.py:33
  26.5 7.6 %gather_fusion = f32[2048,64]{1,0:T(8,128)S(1)} fusion(f32[64,8192]{0,1:T(8,128)} %bitcast.20, s32[2048]{0:T(1024)S(1)} %get-tuple-element.7), kind=kCustom, calls=%fused_computation | custom fusion | bytes 1056768 | tf_op jit(solution)/shard_map/jit(_take)/gather | solution.py:46
  34.2 0.3 copy.16
  34.5 0.8 broadcast_select_fusion
  35.3 6.3 %all-to-all-start = ((f32[64,16,128]{2,0,1:T(8,128)}), f32[64,16,128]{2,0,1:T(8,128)S(1)}, u32[]{:S(2)}, u32[]{:S(2)}) async-start(f32[64,16,128]{2,0,1:T(8,128)} %broadcast_select_fusion), calls=%async_computation | async-start | bytes 1048576 | tf_op jit(solution)/shard_map/all_to_all | solution.py:48
  41.6 0.0 all-reduce.2.cloned.1.call-start
  41.7 0.1 dynamic_slice.6
  41.8 13.3 %all-to-all-done = f32[64,16,128]{2,0,1:T(8,128)S(1)} async-done(((f32[64,16,128]{2,0,1:T(8,128)}), f32[64,16,128]{2,0,1:T(8,128)S(1)}, u32[]{:S(2)}, u32[]{:S(2)}) %all-to-all-start) | async-done | bytes 524320 | tf_op jit(solution)/shard_map/all_to_all | solution.py:48
  55.1 0.1 copy.20
  55.2 0.1 copy.19
  55.3 0.0 copy-start
  55.3 4.7 %all_gather.3 = f32[128,128]{1,0:T(8,128)S(1)} all-gather(f32[64,128]{1,0:T(8,128)S(1)} %copy.19), channel_id=1, replica_groups=mesh['row'=16,'col'=2] {'col'}, dimensions={0}, use_global_device_ids=true | all-gather | bytes 98304 | tf_op jit(solution)/shard_map/all_gather | solution.py:54
  60.0 0.9 fusion.81
  60.9 0.0 all-reduce.2.cloned.1.call-update
  61.0 88.7 %all-reduce.2.cloned.1.call-done = f32[128,128]{1,0:T(8,128)} async-done(((f32[128,128]{1,0:T(8,128)}), f32[128,128]{1,0:T(8,128)}) %all-reduce.2.cloned.1.call-update) | async-done | bytes 65552 | tf_op jit(solution)/shard_map/psum | solution.py:56
  149.6 1.4 dynamic-slice_multiply_fusion
  151.0 0.0 copy-done
  (3 shorter events, 0.1 us)
Async XLA Ops:
  35.3 19.8 %all-to-all-start = ((f32[64,16,128]{2,0,1:T(8,128)}), f32[64,16,128]{2,0,1:T(8,128)S(1)}, u32[]{:S(2)}, u32[]{:S(2)}) async-start(f32[64,16,128]{2,0,1:T(8,128)} %broadcast_select_fusion), calls=%async_computation | async-start | bytes 1048576 | tf_op jit(solution)/shard_map/all_to_all | solution.py:48
  41.6 108.0 %all-reduce.2.cloned.1.call-start = ((), (), s32[]{:S(2)}) async-start(), calls=%async_computation.1 | async-start | bytes 131072 | tf_op jit(solution)/shard_map/psum | solution.py:56
  55.3 95.7 %copy-start = (f32[64,128]{1,0:T(8,128)}, f32[64,128]{1,0:T(8,128)S(1)}, u32[]{:S(2)}) copy-start(f32[64,128]{1,0:T(8,128)S(1)} %copy.19) | copy-start | bytes 98308
Sparse Core Ops, SparseCore 0:
  61.1 88.5 all-reduce.1
where the time goes:
time: 158 us
  waiting for transfers between devices  102 us (65%)
  local copies, waits for them, and re-layouts  19.9 us (13%)
  between operations  14.1 us (9%)
  starting transfers between devices  6.3 us (4%)
  other arithmetic  5.87 us (4%)
  matrix products  4.98 us (3%)
  blocking collectives  4.71 us (3%)
    psum x1, waiting for transfers between devices, body(): totals = lax.psum(partial_gram, 'row')  88.7 us
    all_to_all x1, waiting for transfers between devices, body(): lax.all_to_all(pieces, 'row', split_axis=1, concat_axis=1, tiled=True)  13.3 us
    gather x2, local copies, waits for them, and re-layouts, body(): chosen = jnp.take(mixed, offset, axis=1)  7.96 us
    all_to_all x1, starting transfers between devices, body(): lax.all_to_all(pieces, 'row', split_axis=1, concat_axis=1, tiled=True)  6.27 us
    all_gather x1, blocking collectives, body(): gathered = lax.all_gather(sketch, 'col', axis=0, tiled=True)  4.71 us
    div x1, local copies, waits for them, and re-layouts, local_mix(): return values.reshape(columns, length) / jnp.sqrt(jnp.float32(length))  4.48 us
    reshape x1, local copies, waits for them, and re-layouts, local_mix(): values = values.reshape(columns, first_size, second_size)  4.46 us
  transfers between devices with their start and end apart: 2, of which 2 were waited for; matrix products, arithmetic and copies ran while one was open for 0% of the time, Pallas kernels for 0%

commit v1 on v0

--- a/solution.py
+++ b/solution.py
@@ -53,7 +53,7 @@
     sketch = summed / jnp.sqrt(jnp.float32(devices))
     gathered = lax.all_gather(sketch, "col", axis=0, tiled=True)
     partial_gram = jnp.dot(gathered, gathered.T, precision=lax.Precision.HIGHEST)
-    totals = lax.psum(partial_gram, "row")
+    totals = jnp.sum(lax.all_gather(partial_gram, "row"), axis=0)
     own_rows = lax.dynamic_slice_in_dim(totals, lax.axis_index("col") * columns, columns, 0)
     gram = own_rows / everything
     return (sketch, gram)

time: 158 us -> 109 us (0.69)
  the two profiles are of different devices: /device:TPU:8 before, /device:TPU:0 now
where the time goes in v1:
time: 109 us
  waiting for transfers between devices  51.6 us (47%)
  local copies, waits for them, and re-layouts  19.9 us (18%)
  between operations  14.1 us (13%)
  starting transfers between devices  7.43 us (7%)
  other arithmetic  6.4 us (6%)
  matrix products  4.98 us (5%)
  blocking collectives  4.58 us (4%)
    all_gather x1, waiting for transfers between devices, body(): totals = jnp.sum(lax.all_gather(partial_gram, 'row'), axis=0)  37.5 us
    all_to_all x1, waiting for transfers between devices, body(): lax.all_to_all(pieces, 'row', split_axis=1, concat_axis=1, tiled=True)  14.1 us
    gather x2, local copies, waits for them, and re-layouts, body(): chosen = jnp.take(mixed, offset, axis=1)  7.96 us
    all_to_all x1, starting transfers between devices, body(): lax.all_to_all(pieces, 'row', split_axis=1, concat_axis=1, tiled=True)  7.39 us
    all_gather x1, blocking collectives, body(): gathered = lax.all_gather(sketch, 'col', axis=0, tiled=True)  4.58 us
    div x1, local copies, waits for them, and re-layouts, local_mix(): return values.reshape(columns, length) / jnp.sqrt(jnp.float32(length))  4.48 us
    reshape x1, local copies, waits for them, and re-layouts, local_mix(): values = values.reshape(columns, first_size, second_size)  4.47 us
    mul x1, local copies, waits for them, and re-layouts, local_mix(): values = block.astype(jnp.float32) * signs.astype(jnp.float32)[None, :]  2.7 us
  transfers between devices with their start and end apart: 2, of which 2 were waited for; matrix products, arithmetic and copies ran while one was open for 0% of the time, Pallas kernels for 0%

profile of v1, /device:TPU:0, one launch (start us, length us, event | category | flops | bytes accessed | tf_op | source)
XLA Modules:
  0.0 109.0 jit_solution(8613918768650917385)
XLA Ops:
  7.2 0.7 add_select_fusion
  7.9 0.7 and_bitcast_fusion
  8.6 0.8 convert_element_type.21
  9.4 1.4 %convert_multiply_fusion = f32[64,8192]{1,0:T(8,128)S(1)} fusion(bf16[64,8192]{1,0:T(8,128)(2,1)} %param.3, f32[8192]{0:T(1024)S(1)} %convert_element_type.21), kind=kLoop, calls=%fused_computation.1 | loop fusion | flops 1048576 | bytes 3178496 | tf_op jit(solution)/shard_map/mul | solution.py:25
  10.8 2.7 %copy.13 = f32[64,8192]{0,1:T(8,128)} copy(f32[64,8192]{1,0:T(8,128)S(1)} %convert_multiply_fusion) | data formatting | bytes 4194304 | tf_op jit(solution)/shard_map/mul | solution.py:25
  13.5 4.5 %copy.14 = f32[64,256,32]{1,2,0:T(8,128)S(1)} copy(f32[64,256,32]{0,2,1:T(8,128)} %bitcast.22) | data formatting | bytes 4194304 | tf_op jit(solution)/shard_map/reshape | solution.py:26
  17.9 2.2 %fusion = f32[256,2048]{0,1:S(1)} fusion(f32[256,2048]{0,1:T(8,128)S(1)} %bitcast.23), kind=kOutput, calls=%fused_computation.5 | convolution fusion | flops 1612447744 | bytes 4194304
  20.1 1.9 %convolution_multiply_fusion = f32[64,256,32]{1,2,0:T(8,128)S(1)} fusion(f32[64,256,32]{1,2,0:T(8,128)S(1)} %bitcast.24), kind=kOutput, calls=%fused_computation.2 | convolution fusion | flops 201870336 | bytes 4194304 | tf_op jit(solution)/shard_map/cdb,be->cde/dot_general | solution.py:30
  22.0 4.5 %copy.15 = f32[64,256,32]{0,2,1:T(8,128)} copy(f32[64,256,32]{1,2,0:T(8,128)S(1)} %convolution_multiply_fusion) | data formatting | bytes 4194304 | tf_op jit(solution)/shard_map/div | solution.py:33
  26.5 7.6 %gather_fusion = f32[2048,64]{1,0:T(8,128)S(1)} fusion(f32[64,8192]{0,1:T(8,128)} %bitcast.21, s32[2048]{0:T(1024)S(1)} %get-tuple-element.7), kind=kCustom, calls=%fused_computation | custom fusion | bytes 1056768 | tf_op jit(solution)/shard_map/jit(_take)/gather | solution.py:46
  34.2 0.3 copy.16
  34.5 0.8 broadcast_select_fusion
  35.3 7.4 %all-to-all-start = ((f32[64,16,128]{2,0,1:T(8,128)}), f32[64,16,128]{2,0,1:T(8,128)S(1)}, u32[]{:S(2)}, u32[]{:S(2)}) async-start(f32[64,16,128]{2,0,1:T(8,128)} %broadcast_select_fusion), calls=%async_computation | async-start | bytes 1048576 | tf_op jit(solution)/shard_map/all_to_all | solution.py:48
  42.7 0.0 all-gather.3.cloned.1.call-start
  42.8 0.1 dynamic_slice.6
  42.9 14.1 %all-to-all-done = f32[64,16,128]{2,0,1:T(8,128)S(1)} async-done(((f32[64,16,128]{2,0,1:T(8,128)}), f32[64,16,128]{2,0,1:T(8,128)S(1)}, u32[]{:S(2)}, u32[]{:S(2)}) %all-to-all-start) | async-done | bytes 524320 | tf_op jit(solution)/shard_map/all_to_all | solution.py:48
  57.0 0.1 copy.20
  57.1 0.1 copy.19
  57.2 0.0 copy-start
  57.2 4.6 %all_gather.9 = f32[128,128]{1,0:T(8,128)S(1)} all-gather(f32[64,128]{1,0:T(8,128)S(1)} %copy.19), channel_id=1, replica_groups=mesh['row'=16,'col'=2] {'col'}, dimensions={0}, use_global_device_ids=true | all-gather | bytes 98304 | tf_op jit(solution)/shard_map/all_gather | solution.py:54
  61.8 0.9 fusion.81
  62.7 0.0 all-gather.3.cloned.1.call-update
  62.7 37.5 %all-gather.3.cloned.1.call-done = f32[2048,128]{1,0:T(8,128)} async-done(((f32[128,128]{1,0:T(8,128)}), f32[2048,128]{1,0:T(8,128)}) %all-gather.3.cloned.1.call-update) | async-done | bytes 1048592 | tf_op jit(solution)/shard_map/all_gather | solution.py:56
  100.2 1.3 %reduce_sum.19 = f32[128,128]{1,0:T(8,128)S(1)} reduce(f32[16,128,128]{2,1,0:T(8,128)} %bitcast.26, f32[]{:T(128)} %constant.76.clone.1), dimensions={0}, to_apply=%region_1.2 | reduce | flops 245760 | bytes 1114116 | tf_op jit(solution)/shard_map/reduce_sum | solution.py:56
  101.5 0.6 dynamic-slice_multiply_fusion
  102.1 0.0 copy-done
  (3 shorter events, 0.1 us)
Async XLA Ops:
  35.3 21.7 %all-to-all-start = ((f32[64,16,128]{2,0,1:T(8,128)}), f32[64,16,128]{2,0,1:T(8,128)S(1)}, u32[]{:S(2)}, u32[]{:S(2)}) async-start(f32[64,16,128]{2,0,1:T(8,128)} %broadcast_select_fusion), calls=%async_computation | async-start | bytes 1048576 | tf_op jit(solution)/shard_map/all_to_all | solution.py:48
  42.7 57.5 %all-gather.3.cloned.1.call-start = ((), (), s32[]{:S(2)}) async-start(), calls=%async_computation.1 | async-start | bytes 1114112 | tf_op jit(solution)/shard_map/all_gather | solution.py:56
  57.2 44.9 %copy-start = (f32[64,128]{1,0:T(8,128)}, f32[64,128]{1,0:T(8,128)S(1)}, u32[]{:S(2)}) copy-start(f32[64,128]{1,0:T(8,128)S(1)} %copy.19) | copy-start | bytes 98308
Sparse Core Ops, SparseCore 0:
  62.9 37.3 all-gather.2

commit v2 on v0

--- a/solution.py
+++ b/solution.py
@@ -45,7 +45,10 @@
     offset = sample_rows - owner * length
     chosen = jnp.take(mixed, offset, axis=1)
     pieces = chosen.reshape(columns, devices, per_device)
-    received = lax.all_to_all(pieces, "row", split_axis=1, concat_axis=1, tiled=True)
+    received = jnp.concatenate(
+        lax.all_to_all(jnp.stack(jnp.split(pieces, lax.axis_size("row"), axis=1)), "row", 0, 0),
+        axis=1,
+    )
     mine = lax.dynamic_slice_in_dim(owner, position * per_device, per_device, 0)
     sources = jnp.arange(devices, dtype=jnp.int32)
     table = parity_sign(sources[:, None], mine[None, :], bit_count)

time: 158 us -> 167 us (1.057)
  local copies, waits for them, and re-layouts: 19.9 us -> 29.5 us
    unnamed x4 -> x19, local copies, waits for them, and re-layouts: 0.17 us -> 9.24 us
where the time goes in v2:
time: 167 us
  waiting for transfers between devices  102 us (61%)
  local copies, waits for them, and re-layouts  29.5 us (18%)
  between operations  14.1 us (8%)
  starting transfers between devices  6.3 us (4%)
  other arithmetic  5.08 us (3%)
  matrix products  4.98 us (3%)
  blocking collectives  4.71 us (3%)
    psum x1, waiting for transfers between devices, body(): totals = lax.psum(partial_gram, 'row')  88.7 us
    all_to_all x1, waiting for transfers between devices, body(): lax.all_to_all(jnp.stack(jnp.split(pieces, lax.axis_size('row'), axis=1))...  13.3 us
    unnamed x19, local copies, waits for them, and re-layouts  9.24 us
    gather x2, local copies, waits for them, and re-layouts, body(): chosen = jnp.take(mixed, offset, axis=1)  7.96 us
    all_to_all x1, starting transfers between devices, body(): lax.all_to_all(jnp.stack(jnp.split(pieces, lax.axis_size('row'), axis=1))...  6.27 us
    all_gather x1, blocking collectives, body(): gathered = lax.all_gather(sketch, 'col', axis=0, tiled=True)  4.71 us
    div x1, local copies, waits for them, and re-layouts, local_mix(): return values.reshape(columns, length) / jnp.sqrt(jnp.float32(length))  4.48 us
    reshape x1, local copies, waits for them, and re-layouts, local_mix(): values = values.reshape(columns, first_size, second_size)  4.46 us
  transfers between devices with their start and end apart: 2, of which 2 were waited for; matrix products, arithmetic and copies ran while one was open for 0% of the time, Pallas kernels for 0%

profile of v2, /device:TPU:8, one launch (start us, length us, event | category | flops | bytes accessed | tf_op | source)
XLA Modules:
  0.0 166.7 jit_solution(5680392664026605124)
XLA Ops:
  7.2 0.7 add_select_fusion
  7.9 0.7 and_bitcast_fusion
  8.6 0.8 convert_element_type.21
  9.4 1.4 convert_multiply_fusion
  10.8 2.7 %copy.13 = f32[64,8192]{0,1:T(8,128)} copy(f32[64,8192]{1,0:T(8,128)S(1)} %convert_multiply_fusion) | data formatting | bytes 4194304 | tf_op jit(solution)/shard_map/mul | solution.py:25
  13.5 4.5 %copy.14 = f32[64,256,32]{1,2,0:T(8,128)S(1)} copy(f32[64,256,32]{0,2,1:T(8,128)} %bitcast.91) | data formatting | bytes 4194304 | tf_op jit(solution)/shard_map/reshape | solution.py:26
  17.9 2.2 %fusion.1 = f32[256,2048]{0,1:S(1)} fusion(f32[256,2048]{0,1:T(8,128)S(1)} %bitcast.92), kind=kOutput, calls=%fused_computation.6 | convolution fusion | flops 1612447744 | bytes 4194304
  20.1 1.9 %convolution_multiply_fusion = f32[64,256,32]{1,2,0:T(8,128)S(1)} fusion(f32[64,256,32]{1,2,0:T(8,128)S(1)} %bitcast.93), kind=kOutput, calls=%fused_computation.2 | convolution fusion | flops 201870336 | bytes 4194304 | tf_op jit(solution)/shard_map/cdb,be->cde/dot_general | solution.py:30
  22.0 4.5 %copy.15 = f32[64,256,32]{0,2,1:T(8,128)} copy(f32[64,256,32]{1,2,0:T(8,128)S(1)} %convolution_multiply_fusion) | data formatting | bytes 4194304 | tf_op jit(solution)/shard_map/div | solution.py:33
  26.5 7.6 %gather_fusion = f32[2048,64]{1,0:T(8,128)S(1)} fusion(f32[64,8192]{0,1:T(8,128)} %bitcast.90, s32[2048]{0:T(1024)S(1)} %get-tuple-element.7), kind=kCustom, calls=%fused_computation | custom fusion | bytes 1056768 | tf_op jit(solution)/shard_map/jit(_take)/gather | solution.py:46
  34.5 0.6 fusion.55
  35.2 0.6 fusion.54
  35.8 0.6 fusion.53
  36.4 0.6 fusion.52
  37.0 0.6 fusion.51
  37.6 0.6 fusion.50
  38.2 0.6 fusion.49
  38.8 0.6 fusion.48
  39.4 0.6 fusion.47
  40.0 0.6 fusion.46
  40.6 0.6 fusion.45
  41.2 0.6 fusion.44
  41.8 0.6 fusion.43
  42.4 0.6 fusion.42
  43.0 0.6 fusion.41
  43.6 0.6 fusion.40
  44.2 6.3 %all-to-all-start = ((f32[16,64,1,128]{3,1,2,0:T(8,128)}), f32[16,64,1,128]{3,1,2,0:T(8,128)S(1)}, u32[]{:S(2)}, u32[]{:S(2)}) async-start(f32[16,64,1,128]{3,1,2,0:T(8,128)} %fusion.40), calls=%async_computation | async-start | bytes 1048576 | tf_op jit(solution)/shard_map/all_to_all | solution.py:49
  50.7 13.3 %all-to-all-done = f32[16,64,1,128]{3,1,2,0:T(8,128)S(1)} async-done(((f32[16,64,1,128]{3,1,2,0:T(8,128)}), f32[16,64,1,128]{3,1,2,0:T(8,128)S(1)}, u32[]{:S(2)}, u32[]{:S(2)}) %all-to-all-start) | async-done | bytes 524320 | tf_op jit(solution)/shard_map/all_to_all | solution.py:49
  64.2 4.7 %all_gather.3 = f32[128,128]{1,0:T(8,128)S(1)} all-gather(f32[64,128]{1,0:T(8,128)S(1)} %copy.19), channel_id=1, replica_groups=mesh['row'=16,'col'=2] {'col'}, dimensions={0}, use_global_device_ids=true | all-gather | bytes 98304 | tf_op jit(solution)/shard_map/all_gather | solution.py:57
  68.9 0.9 fusion.98
  69.9 88.7 %all-reduce.2.cloned.1.call-done = f32[128,128]{1,0:T(8,128)} async-done(((f32[128,128]{1,0:T(8,128)}), f32[128,128]{1,0:T(8,128)}) %all-reduce.2.cloned.1.call-update) | async-done | bytes 65552 | tf_op jit(solution)/shard_map/psum | solution.py:59
  158.5 1.4 dynamic-slice_multiply_fusion
  (12 shorter events, 0.7 us)
Async XLA Ops:
  44.2 19.8 %all-to-all-start = ((f32[16,64,1,128]{3,1,2,0:T(8,128)}), f32[16,64,1,128]{3,1,2,0:T(8,128)S(1)}, u32[]{:S(2)}, u32[]{:S(2)}) async-start(f32[16,64,1,128]{3,1,2,0:T(8,128)} %fusion.40), calls=%async_computation | async-start | bytes 1048576 | tf_op jit(solution)/shard_map/all_to_all | solution.py:49
  50.5 108.0 %all-reduce.2.cloned.1.call-start = ((), (), s32[]{:S(2)}) async-start(), calls=%async_computation.1 | async-start | bytes 131072 | tf_op jit(solution)/shard_map/psum | solution.py:59
  64.2 95.7 %copy-start = (f32[64,128]{1,0:T(8,128)}, f32[64,128]{1,0:T(8,128)S(1)}, u32[]{:S(2)}) copy-start(f32[64,128]{1,0:T(8,128)S(1)} %copy.19) | copy-start | bytes 98308
Sparse Core Ops, SparseCore 0:
  70.0 88.5 all-reduce.1
